TPU v7x, 32 devices: a whole 2x2x4 slice. The times are simulated.
32 devices in a mesh: tm: 8 (over z, y), mp: 4 (over x, core).
Axes of the slice: x: 2, y: 2, z: 4, core: 2. Of those that a mesh axis runs over, the one named last changes fastest.
Arguments:
- queries: bfloat16 [1536, 1024], P('tm', 'mp'), may hold values from -8 to 8
- d_queries: bfloat16 [1536, 1024], P('tm', 'mp'), may hold values from -6 to 6
- key_rows: bfloat16 [1536, 1024], P('tm', 'mp'), may hold values from -8 to 8
- value_rows: bfloat16 [1536, 1024], P('tm', 'mp'), may hold values from -6 to 6
- d_key_rows: bfloat16 [1536, 1024], P('tm', 'mp'), may hold values from -6 to 6
- d_value_rows: bfloat16 [1536, 1024], P('tm', 'mp'), may hold values from -6 to 6
- live_flags: int32 [1536], P('tm'), may hold values from 0 to 1, as said below
- out_weight: bfloat16 [1024, 5120], P('mp'), may hold values from -1 to 1
- gate_scale: float32 [5120], P('mp'), may hold values from 0.25 to 1.75
- tokens: bfloat16 [1536, 5120], P('tm', 'mp'), may hold values from -6 to 6
- d_tokens: bfloat16 [1536, 5120], P('tm', 'mp'), may hold values from -6 to 6
Outputs:
- result: bfloat16 [1536, 5120], P('tm', 'mp')
- d_result: bfloat16 [1536, 5120], P('tm', 'mp')
Inputs may be any that keep to these rules, and one draw needn't show every extreme that they name: live_flags are equal within each aligned run of 32 tokens.
All inputs are finite; a program needn't handle non-finite values.
Results may differ from a plain program's by a relative error of at most 0.019.
Values may be sent and summed in bfloat16 or wider, within the bound.
A program may use at most 128 MiB of HBM per device.

v0:
```python
import math

import jax
import jax.numpy as jnp
from jax import lax
from jax.sharding import PartitionSpec as P

HD = 128


def by_heads(matrix):
    return matrix.reshape(matrix.shape[0], matrix.shape[1] // HD, HD)


def attend(running, pieces, queries_h, tangent_h):
    keys_h, values_h, dkeys_h, dvalues_h = [by_heads(matrix) for matrix in pieces]
    factor = 1.0 / math.sqrt(HD)
    scores = (
        jnp.einsum("qhd,khd->qhk", queries_h, keys_h, preferred_element_type=jnp.float32) * factor
    )
    d_scores = (
        jnp.einsum("qhd,khd->qhk", tangent_h, keys_h, preferred_element_type=jnp.float32)
        + jnp.einsum("qhd,khd->qhk", queries_h, dkeys_h, preferred_element_type=jnp.float32)
    ) * factor
    peak_old, totals, slopes, primal, tangent = running
    peak_new = jnp.max(scores, axis=2)
    rescale = jnp.exp(peak_old - peak_new)
    weights = jnp.exp(scores - peak_new[:, :, None])
    product = weights * d_scores
    weights_b = weights.astype(jnp.bfloat16)
    product_b = product.astype(jnp.bfloat16)
    totals = totals * rescale + jnp.sum(weights, axis=2)
    slopes = slopes * rescale + jnp.sum(product, axis=2)
    primal = primal * rescale[:, :, None] + jnp.einsum(
        "qhk,khd->qhd", weights_b, values_h, preferred_element_type=jnp.float32
    )
    tangent = (
        tangent * rescale[:, :, None]
        + jnp.einsum("qhk,khd->qhd", product_b, values_h, preferred_element_type=jnp.float32)
        + jnp.einsum("qhk,khd->qhd", weights_b, dvalues_h, preferred_element_type=jnp.float32)
    )
    return (peak_new, totals, slopes, primal, tangent)


def per_device(
    queries,
    d_queries,
    key_rows,
    value_rows,
    d_key_rows,
    d_value_rows,
    live_flags,
    out_weight,
    gate_scale,
    tokens,
    d_tokens,
):
    live_rows = live_flags[:, None] > 0

    def masked(matrix):
        return jnp.where(live_rows, matrix, jnp.zeros_like(matrix))

    tangent_q = masked(d_queries)
    tangent_k = masked(d_key_rows)
    tangent_v = masked(d_value_rows)
    tangent_x = masked(d_tokens)
    queries_h = by_heads(queries)
    tangent_h = by_heads(tangent_q)
    row_count = queries.shape[0]
    head_count = queries.shape[1] // HD
    initial = (
        jnp.full((row_count, head_count), -jnp.inf, jnp.float32),
        jnp.zeros((row_count, head_count), jnp.float32),
        jnp.zeros((row_count, head_count), jnp.float32),
        jnp.zeros((row_count, head_count, HD), jnp.float32),
        jnp.zeros((row_count, head_count, HD), jnp.float32),
    )
    finished = attend(
        initial,
        (
            lax.all_gather(key_rows, "tm", axis=0, tiled=True),
            lax.all_gather(value_rows, "tm", axis=0, tiled=True),
            lax.all_gather(tangent_k, "tm", axis=0, tiled=True),
            lax.all_gather(tangent_v, "tm", axis=0, tiled=True),
        ),
        queries_h,
        tangent_h,
    )
    peak_new, totals, slopes, primal, tangent = finished
    outputs = primal / totals[:, :, None]
    d_outputs = tangent / totals[:, :, None] - (slopes / totals)[:, :, None] * outputs
    outputs_b = outputs.astype(jnp.bfloat16).reshape(row_count, head_count * HD)
    d_outputs_b = d_outputs.astype(jnp.bfloat16).reshape(row_count, head_count * HD)
    partial_y = jnp.dot(outputs_b, out_weight, preferred_element_type=jnp.float32)
    partial_dy = jnp.dot(d_outputs_b, out_weight, preferred_element_type=jnp.float32)
    summed, d_summed = (
        lax.psum_scatter(
            partial_y.astype(jnp.bfloat16), "mp", scatter_dimension=1, tiled=True
        ).astype(jnp.float32),
        lax.psum_scatter(
            partial_dy.astype(jnp.bfloat16), "mp", scatter_dimension=1, tiled=True
        ).astype(jnp.float32),
    )
    result = (tokens.astype(jnp.float32) + gate_scale * summed).astype(jnp.bfloat16)
    d_result = (tangent_x.astype(jnp.float32) + gate_scale * d_summed).astype(jnp.bfloat16)
    return (result, d_result)


def solution(mesh):
    placed = (
        P("tm", "mp"),
        P("tm", "mp"),
        P("tm", "mp"),
        P("tm", "mp"),
        P("tm", "mp"),
        P("tm", "mp"),
        P("tm"),
        P("mp", None),
        P("mp"),
        P("tm", "mp"),
        P("tm", "mp"),
    )
    return jax.shard_map(
        per_device,
        mesh=mesh,
        in_specs=placed,
        out_specs=(P("tm", "mp"), P("tm", "mp")),
        check_vma=False,
    )
```

profile of v0, /device:TPU:0, one launch (start us, length us, event | category | flops | bytes accessed | tf_op | source)
XLA Modules:
  0.0 231.6 jit_solution(13017451342450067046)
XLA Ops:
  7.2 0.0 copy-start
  7.2 0.0 reduce-scatter.5.cloned.1.call-start
  7.2 36.4 %all_gather.12 = bf16[1536,256]{1,0:T(8,128)(2,1)} all-gather(bf16[192,256]{1,0:T(8,128)(2,1)} %param.13), channel_id=1, replica_groups=mesh['tm'=8,'mp'=4] {'tm'}, dimensions={0}, use_global_device_ids=true | all-gather | bytes 884736 | tf_op jit(solution)/shard_map/all_gather | solution.py:81
  43.6 1.4 copy.32
  45.0 0.0 copy-start.7
  45.0 0.0 copy-start.8
  45.1 0.0 copy-start.9
  45.1 1.9 fusion.44
  47.0 0.7 broadcast_select_fusion.1
  47.7 1.9 convolution_bitcast_fusion.1
  49.6 32.0 %all_gather.14 = bf16[1536,256]{1,0:T(8,128)(2,1)S(1)} all-gather(bf16[192,256]{1,0:T(8,128)(2,1)S(1)} %get-tuple-element.7), channel_id=1, replica_groups=mesh['tm'=8,'mp'=4] {'tm'}, dimensions={0}, use_global_device_ids=true | all-gather | bytes 884736 | tf_op jit(solution)/shard_map/all_gather | solution.py:83
  81.6 1.2 copy.40
  82.7 32.0 %all_gather.13 = bf16[1536,256]{1,0:T(8,128)(2,1)S(1)} all-gather(bf16[192,256]{1,0:T(8,128)(2,1)} %param.14), channel_id=1, replica_groups=mesh['tm'=8,'mp'=4] {'tm'}, dimensions={0}, use_global_device_ids=true | all-gather | bytes 884736 | tf_op jit(solution)/shard_map/all_gather | solution.py:82
  114.8 1.2 copy.35
  116.0 32.2 %all_gather.15 = bf16[1536,256]{1,0:T(8,128)(2,1)S(1)} all-gather(bf16[192,256]{1,0:T(8,128)(2,1)} %get-tuple-element.8), channel_id=1, replica_groups=mesh['tm'=8,'mp'=4] {'tm'}, dimensions={0}, use_global_device_ids=true | all-gather | bytes 884736 | tf_op jit(solution)/shard_map/all_gather | solution.py:84
  148.1 1.2 copy.44
  149.3 2.3 fusion.4
  151.6 0.1 copy-done.1
  151.7 1.7 convolution_bitcast_fusion.2
  153.4 0.9 fusion.45
  154.3 0.2 copy-done.4
  154.5 0.6 fusion.24
  155.1 0.5 fusion.28
  155.6 2.0 convolution_convert_fusion
  157.6 0.0 reduce-scatter.5.cloned.1.call-update
  157.6 0.0 copy-start.5
  157.6 0.0 reduce-scatter.3.cloned.1.call-start
  157.7 2.0 convolution_convert_fusion.1
  159.6 0.0 reduce-scatter.3.cloned.1.call-update
  159.6 29.5 %reduce-scatter.5.cloned.1.call-done = bf16[192,1280]{1,0:T(8,128)(2,1)} async-done(((bf16[192,5120]{1,0:T(8,128)(2,1)}), bf16[192,1280]{1,0:T(8,128)(2,1)}) %reduce-scatter.5.cloned.1.call-update) | async-done | bytes 491536 | tf_op jit(solution)/shard_map/reduce_scatter | solution.py:100
  189.2 33.0 %reduce-scatter.3.cloned.1.call-done = bf16[192,1280]{1,0:T(8,128)(2,1)} async-done(((bf16[192,5120]{1,0:T(8,128)(2,1)}), bf16[192,1280]{1,0:T(8,128)(2,1)}) %reduce-scatter.3.cloned.1.call-update) | async-done | bytes 491536 | tf_op jit(solution)/shard_map/reduce_scatter | solution.py:97
  222.2 2.6 %add_convert_fusion = (bf16[192,1280]{1,0:T(8,128)(2,1)}, bf16[192,1280]{1,0:T(8,128)(2,1)}) fusion(bf16[192,1280]{1,0:T(8,128)(2,1)} %reduce-scatter.5.cloned.1.call-done, bf16[192,1280]{1,0:T(8,128)(2,1)S(1)} %copy-done.5, f32[1280]{0:T(1024)S(1)} %copy-done.10, pred[192]{0:T(512)(128)(4,1)S(1)} %broadcast_compare_fusion, ...), kind=kLoop, calls=%fused_computation.25 | loop fusion | flops 2703360 | bytes 2954432 | tf_op jit(solution)/shard_map/convert_element_type | solution.py:105
  (19 shorter events, 0.1 us)
Async XLA Ops:
  7.2 148.4 %copy-start = (bf16[256,5120]{1,0:T(8,128)(2,1)S(1)}, bf16[256,5120]{1,0:T(8,128)(2,1)}, u32[]{:S(2)}) copy-start(bf16[256,5120]{1,0:T(8,128)(2,1)} %param.18) | copy-start | bytes 7864324
  7.2 37.8 %copy-start.11 = (s32[192]{0:T(256)S(1)}, s32[192]{0:T(256)}, u32[]{:S(2)}) copy-start(s32[192]{0:T(256)} %param.17) | copy-start | bytes 2308
  7.2 37.9 %copy-start.6 = (bf16[192,256]{1,0:T(8,128)(2,1)S(1)}, bf16[192,256]{1,0:T(8,128)(2,1)}, u32[]{:S(2)}) copy-start(bf16[192,256]{1,0:T(8,128)(2,1)} %param.11) | copy-start | bytes 294916
  7.2 182.0 %reduce-scatter.5.cloned.1.call-start = ((), (), s32[]{:S(2)}) async-start(), calls=%async_computation.3 | async-start | bytes 2457600 | tf_op jit(solution)/shard_map/reduce_scatter | solution.py:100
  45.0 1.9 copy-start.7
  45.0 1.9 copy-start.8
  45.1 1.9 copy-start.9
  149.3 2.4 %copy-start.1 = (f32[192,2,1536]{2,0,1:T(8,128)S(1)}, f32[192,2,1536]{2,0,1:T(8,128)}, u32[]{:S(2)}) copy-start(f32[192,2,1536]{2,0,1:T(8,128)} %get-tuple-element.11) | copy-start | bytes 7077892
  149.3 4.0 %copy-start.2 = (f32[192,2,1536]{2,0,1:T(8,128)S(1)}, f32[192,2,1536]{2,0,1:T(8,128)}, u32[]{:S(2)}) copy-start(f32[192,2,1536]{2,0,1:T(8,128)} %convolution_bitcast_fusion.1) | copy-start | bytes 7077892
  149.3 4.0 %copy-start.3 = (bf16[1536,256]{0,1:T(8,128)(2,1)S(1)}, bf16[1536,256]{0,1:T(8,128)(2,1)}, u32[]{:S(2)}) copy-start(bf16[1536,256]{0,1:T(8,128)(2,1)} %copy.40) | copy-start | bytes 2359300
  153.4 1.1 copy-start.4
  157.6 64.6 %copy-start.5 = (bf16[192,1280]{1,0:T(8,128)(2,1)S(1)}, bf16[192,1280]{1,0:T(8,128)(2,1)}, u32[]{:S(2)}) copy-start(bf16[192,1280]{1,0:T(8,128)(2,1)} %param.21) | copy-start | bytes 1474564
  157.6 64.6 %copy-start.10 = (f32[1280]{0:T(1024)S(1)}, f32[1280]{0:T(1024)}, u32[]{:S(2)}) copy-start(f32[1280]{0:T(1024)} %param.19) | copy-start | bytes 15364
  157.6 64.5 %reduce-scatter.3.cloned.1.call-start = ((), (), s32[]{:S(2)}) async-start(), calls=%async_computation.2 | async-start | bytes 2457600 | tf_op jit(solution)/shard_map/reduce_scatter | solution.py:97
Sparse Core Ops, SparseCore 0:
  157.7 31.4 reduce-scatter.4
  191.7 30.3 reduce-scatter.2
where the time goes:
time: 232 us
  blocking collectives  133 us (57%)
  waiting for transfers between devices  62.5 us (27%)
  between operations  14.2 us (6%)
  matrix products  11.3 us (5%)
  other arithmetic  5.65 us (2%)
  local copies, waits for them, and re-layouts  5.29 us (2%)
    all_gather x1, blocking collectives, per_device(): lax.all_gather(key_rows, 'tm', axis=0, tiled=True)  36.4 us
    reduce_scatter x1, waiting for transfers between devices, per_device(): lax.psum_scatter(partial_y.astype(jnp.bfloat16), 'mp', scatter_dimension=...  33 us
    all_gather x1, blocking collectives, per_device(): lax.all_gather(tangent_v, 'tm', axis=0, tiled=True)  32.2 us
    all_gather x1, blocking collectives, per_device(): lax.all_gather(value_rows, 'tm', axis=0, tiled=True)  32 us
    all_gather x1, blocking collectives, per_device(): lax.all_gather(tangent_k, 'tm', axis=0, tiled=True)  32 us
    reduce_scatter x1, waiting for transfers between devices, per_device(): lax.psum_scatter(partial_dy.astype(jnp.bfloat16), 'mp', scatter_dimension...  29.5 us
  transfers between devices with their start and end apart: 2, of which 2 were waited for; matrix products, arithmetic and copies ran while one was open for 1% of the time, Pallas kernels for 0%

commit v1 on v0

v1 whole, which is shorter than its diff:
```python
import functools
import math

import jax
import jax.numpy as jnp
from jax import lax
from jax.experimental import pallas as pl
from jax.experimental.pallas import tpu as pltpu
from jax.sharding import PartitionSpec as P

HD = 128
FRAME = 32
MESH = pl.DeviceIdType.MESH
F32 = jnp.float32
BF16 = jnp.bfloat16


def ring_place(t, n):
    return jnp.where(t % 2 == 0, t // 2, n - 1 - t // 2)


def ring_member(r, n):
    return jnp.where(r < n // 2, 2 * r, 2 * (n - 1 - r) + 1)


def flipped(me, j):
    other = me
    bit = 1
    while bit <= j:
        if j & bit:
            other = other + bit * (1 - 2 * ((me // bit) % 2))
        bit *= 2
    return other


def dot_nt(a, b):
    return lax.dot_general(a, b, (((1,), (1,)), ((), ())), preferred_element_type=F32)


def dot_nn(a, b):
    return lax.dot_general(a, b, (((1,), (0,)), ((), ())), preferred_element_type=F32)


def fused(
    n,
    n_mp,
    move_w,
    q_hbm,
    dq_hbm,
    k_hbm,
    v_hbm,
    dk_hbm,
    dv_hbm,
    flags,
    w_hbm,
    gate,
    x_hbm,
    dx_hbm,
    out,
    d_out,
    own,
    qcat,
    tkv,
    kv,
    opp,
    m_s,
    l_s,
    c_s,
    a_s,
    g_s,
    ao,
    wbuf,
    acc,
    xbuf,
    own_sem,
    x_sem,
    w_local,
    ks,
    kr,
    ws,
    wr,
    as_,
    ar,
):
    rows, width = q_hbm.shape
    heads = width // HD
    cols = out.shape[1]
    half = n // 2
    t = lax.axis_index("tm")
    m = lax.axis_index("mp")
    place = ring_place(t, n)
    right = ring_member((place + 1) % n, n)
    left = ring_member((place + n - 1) % n, n)
    peers = [flipped(m, j) for j in range(n_mp)]
    factor = 1.0 / math.sqrt(HD)

    def lanes(h):
        return slice(h * HD, (h + 1) * HD)

    loads = [
        pltpu.make_async_copy(src, own.at[i], own_sem.at[i])
        for i, src in enumerate((k_hbm, v_hbm, dk_hbm, dv_hbm, q_hbm, dq_hbm))
    ]
    for load in loads:
        load.start()

    barrier = pltpu.get_barrier_semaphore()
    for dev in [(right, m), (left, m)] + [(t, peers[j]) for j in range(1, n_mp)]:
        pl.semaphore_signal(barrier, inc=1, device_id=dev, device_id_type=MESH)
    pl.semaphore_wait(barrier, 1 + n_mp)

    def exists(d, s, p):
        return s < half or (s == half and (p < 2) == (d == 0))

    def kv_copy(h, d, s, p):
        side = slice(d * rows, (d + 1) * rows)
        if s > 1:
            src = kv.at[h, s - 2, p, side]
        elif p < 2:
            src = (k_hbm, v_hbm)[p].at[:, lanes(h)]
        else:
            src = tkv.at[h, p - 2]
        dst = kv.at[h, s - 1, p, side] if s < half else opp.at[h, p]
        return pltpu.make_async_remote_copy(
            src_ref=src,
            dst_ref=dst,
            send_sem=ks.at[h, d, s - 1, p],
            recv_sem=kr.at[h, d, s - 1, p],
            device_id=((right, left)[d], m),
            device_id_type=MESH,
        )

    def send_own(h, pieces):
        for p in pieces:
            for d in (0, 1):
                kv_copy(h, d, 1, p).start()

    def w_copy(h, j):
        span = pl.ds(pl.multiple_of(peers[j] * cols, HD), cols)
        part = slice(h * HD, (h + 1) * HD)
        if j == 0:
            return pltpu.make_async_copy(
                w_hbm.at[part, span], wbuf.at[0, part], w_local.at[h]
            )
        return pltpu.make_async_remote_copy(
            src_ref=w_hbm.at[part, span],
            dst_ref=wbuf.at[j, part],
            send_sem=ws.at[h, j],
            recv_sem=wr.at[h, j],
            device_id=(t, peers[j]),
            device_id_type=MESH,
        )

    def ao_copy(h, j):
        relay = j % 2 == 1 and j > 1
        return pltpu.make_async_remote_copy(
            src_ref=ao.at[h, j - 1 if relay else 0],
            dst_ref=ao.at[h, j],
            send_sem=as_.at[h, j],
            recv_sem=ar.at[h, j],
            device_id=(t, peers[1] if relay else peers[j]),
            device_id_type=MESH,
        )

    send_own(0, (0, 1))
    if move_w:
        for h in range(heads):
            for j in list(range(2, n_mp)) + [1, 0]:
                w_copy(h, j).start()
    x_loads = [
        pltpu.make_async_copy(src, xbuf.at[i], x_sem.at[i])
        for i, src in enumerate((x_hbm, dx_hbm))
    ]
    for load in x_loads:
        load.start()
    for load in loads:
        load.wait()

    live = [
        jnp.where(flags[i * FRAME] > 0, 1.0, 0.0).astype(F32)
        for i in range(rows // FRAME)
    ]

    def masked(value, i):
        scale = jnp.full(value.shape, live[i], F32)
        return (value.astype(F32) * scale).astype(BF16)

    for h in range(heads):
        for i in range(rows // FRAME):
            part = slice(i * FRAME, (i + 1) * FRAME)
            tkv[h, 0, part] = masked(own[2, part, lanes(h)], i)
            tkv[h, 1, part] = masked(own[3, part, lanes(h)], i)
        if h == 0:
            send_own(0, (2, 3))
    for h in range(heads):
        for i in range(rows // FRAME):
            part = slice(i * FRAME, (i + 1) * FRAME)
            qcat[h, part, 0:HD] = masked(own[5, part, lanes(h)], i)
        qcat[h, :, HD : 2 * HD] = own[4, :, lanes(h)]

    def attend(h, k, v, tk, tv, first):
        queries = qcat[h, :, HD : 2 * HD]
        scores = dot_nt(queries, k)
        d_scores = dot_nt(qcat[h], jnp.concatenate([k, tk], axis=1)) * factor
        peak = jnp.max(scores, axis=1, keepdims=True)
        if not first:
            peak_old = m_s[...]
            peak = jnp.maximum(peak_old, peak)
            rescale = jnp.exp((peak_old - peak) * factor)
        weights = jnp.exp((scores - peak) * factor)
        product = weights * d_scores
        total = jnp.sum(weights, axis=1, keepdims=True)
        slope = jnp.sum(product, axis=1, keepdims=True)
        weights_b = weights.astype(BF16)
        product_b = product.astype(BF16)
        primal = dot_nn(weights_b, v)
        tangent = dot_nn(product_b, v) + dot_nn(weights_b, tv)
        m_s[...] = peak
        if first:
            l_s[...] = total
            c_s[...] = slope
            a_s[...] = primal
            g_s[...] = tangent
        else:
            l_s[...] = l_s[...] * rescale + total
            c_s[...] = c_s[...] * rescale + slope
            a_s[...] = a_s[...] * rescale + primal
            g_s[...] = g_s[...] * rescale + tangent

    def finish(h):
        inverse = 1.0 / l_s[...]
        outputs = a_s[...] * inverse
        d_outputs = g_s[...] * inverse - (c_s[...] * inverse) * outputs
        ao[h, 0, 0:rows] = outputs.astype(BF16)
        ao[h, 0, rows : 2 * rows] = d_outputs.astype(BF16)
        for j in list(range(2, n_mp, 2)) + [1]:
            ao_copy(h, j).start()

    def relay(h):
        for j in range(2, n_mp, 2):
            ao_copy(h, j).wait_recv()
            ao_copy(h, j + 1).start()

    for h in range(heads):
        attend(h, own[0, :, lanes(h)], own[1, :, lanes(h)], tkv[h, 0], tkv[h, 1], True)
        for s in range(1, half):
            for p in range(4):
                for d in (0, 1):
                    kv_copy(h, d, s, p).wait_recv()
                    if exists(d, s + 1, p):
                        kv_copy(h, d, s + 1, p).start()
            if h + 1 < heads:
                if s == 1:
                    send_own(h + 1, (0, 1))
                if s == min(2, half - 1):
                    send_own(h + 1, (2, 3))
            attend(h, *[kv[h, s - 1, p] for p in range(4)], False)
        if h > 0:
            relay(h - 1)
        for p in range(4):
            kv_copy(h, 0 if p < 2 else 1, half, p).wait_recv()
        attend(h, *[opp[h, p] for p in range(4)], False)
        finish(h)

    step = 2 * HD if cols % (2 * HD) == 0 else cols
    chunks = [slice(c, c + step) for c in range(0, cols, step)]

    def w_part(h, j, chunk):
        part = slice(h * HD, (h + 1) * HD)
        if move_w:
            return wbuf[j, part, chunk]
        return w_hbm[peers[j], part, chunk]

    def project(h, slots, chunk):
        attn = jnp.concatenate([ao[h, j] for j in slots], axis=1)
        weight = jnp.concatenate([w_part(h, j, chunk) for j in slots], axis=0)
        return dot_nn(attn, weight)

    near = (0, 1)
    far = tuple(range(2, n_mp))
    last = heads - 1
    for h in range(last):
        for j in range(1, n_mp):
            if j % 2 == 1:
                ao_copy(h, j).wait_recv()
            if move_w:
                w_copy(h, j).wait_recv()
        if move_w:
            w_copy(h, 0).wait()
        for chunk in chunks:
            part = project(h, near + far, chunk)
            acc[:, chunk] = part if h == 0 else acc[:, chunk] + part
    ao_copy(last, 1).wait_recv()
    if move_w:
        w_copy(last, 0).wait()
        for j in range(1, n_mp):
            w_copy(last, j).wait_recv()
    for chunk in chunks:
        part = project(last, near, chunk)
        acc[:, chunk] = part if last == 0 else acc[:, chunk] + part
    for load in x_loads:
        load.wait()
    relay(last)
    for j in range(3, n_mp, 2):
        ao_copy(last, j).wait_recv()
    for chunk in chunks:
        part = acc[:, chunk] + project(last, far, chunk)
        scale = gate[:, chunk]
        out[:, chunk] = (xbuf[0, :, chunk].astype(F32) + scale * part[0:rows]).astype(BF16)
        for i in range(rows // FRAME):
            piece = slice(i * FRAME, (i + 1) * FRAME)
            base = xbuf[1, piece, chunk].astype(F32)
            base = base * jnp.full(base.shape, live[i], F32)
            delta = part[rows + i * FRAME : rows + (i + 1) * FRAME]
            d_out[piece, chunk] = (base + scale * delta).astype(BF16)

    for h in range(heads):
        for s in range(1, half + 1):
            for p in range(4):
                for d in (0, 1):
                    if exists(d, s, p):
                        kv_copy(h, d, s, p).wait_send()
        for j in range(1, n_mp):
            ao_copy(h, j).wait_send()
            if move_w:
                w_copy(h, j).wait_send()


def per_device(n, n_mp, q, dq, k, v, dk, dv, flags, w, gate, x, dx):
    rows, width = q.shape
    cols = x.shape[1]
    heads = width // HD
    half = n // 2
    move_w = cols % HD == 0
    if not move_w:
        w = lax.all_to_all(w, "mp", split_axis=1, concat_axis=0, tiled=True)
        w = w.reshape(n_mp, width, cols)
    anywhere = pl.BlockSpec(memory_space=pl.ANY)
    vmem = pl.BlockSpec(memory_space=pltpu.VMEM)
    dma = pltpu.SemaphoreType.DMA
    return pl.pallas_call(
        functools.partial(fused, n, n_mp, move_w),
        out_shape=(jax.ShapeDtypeStruct(x.shape, BF16), jax.ShapeDtypeStruct(x.shape, BF16)),
        in_specs=[anywhere] * 6
        + [pl.BlockSpec(memory_space=pltpu.SMEM), anywhere if move_w else vmem, vmem]
        + [anywhere] * 2,
        out_specs=(vmem, vmem),
        scratch_shapes=[
            pltpu.VMEM((6, rows, width), BF16),
            pltpu.VMEM((heads, rows, 2 * HD), BF16),
            pltpu.VMEM((heads, 2, rows, HD), BF16),
            pltpu.VMEM((heads, half - 1, 4, 2 * rows, HD), BF16),
            pltpu.VMEM((heads, 4, rows, HD), BF16),
            pltpu.VMEM((rows, 1), F32),
            pltpu.VMEM((rows, 1), F32),
            pltpu.VMEM((rows, 1), F32),
            pltpu.VMEM((rows, HD), F32),
            pltpu.VMEM((rows, HD), F32),
            pltpu.VMEM((heads, n_mp, 2 * rows, HD), BF16),
            pltpu.VMEM((n_mp, width, cols) if move_w else (1, 16, HD), BF16),
            pltpu.VMEM((2 * rows, cols), F32),
            pltpu.VMEM((2, rows, cols), BF16),
            dma((6,)),
            dma((2,)),
            dma((heads,)),
            dma((heads, 2, half, 4)),
            dma((heads, 2, half, 4)),
            dma((heads, n_mp)),
            dma((heads, n_mp)),
            dma((heads, n_mp)),
            dma((heads, n_mp)),
        ],
        compiler_params=pltpu.CompilerParams(
            collective_id=0, has_side_effects=True, vmem_limit_bytes=48 * 1024 * 1024
        ),
    )(q, dq, k, v, dk, dv, flags, w, gate.reshape(1, cols), x, dx)


def solution(mesh):
    both = P("tm", "mp")
    placed = (both,) * 6 + (P("tm"), P("mp", None), P("mp"), both, both)
    return jax.shard_map(
        functools.partial(per_device, mesh.shape["tm"], mesh.shape["mp"]),
        mesh=mesh,
        in_specs=placed,
        out_specs=(both, both),
        check_vma=False,
    )
```

time: 232 us -> 61.6 us (0.27)
  blocking collectives: 133 us -> 0 us
  waiting for transfers between devices: 62.5 us -> 0 us
  Pallas kernels: 0 us -> 47.9 us
  between operations: 14.2 us -> 0.65 us
  matrix products: 11.3 us -> 0 us
  local copies, waits for them, and re-layouts: 5.29 us -> 12.1 us
  other arithmetic: 5.65 us -> 0 us
    all_gather x4 -> x0, blocking collectives: 133 us -> none  [the longest x1 36.4 us: per_device(): lax.all_gather(key_rows, 'tm', axis=0, tiled=True)]
    reduce_scatter x2 -> x0, waiting for transfers between devices: 62.5 us -> none  [the longest x1 33 us: per_device(): lax.psum_scatter(partial_y.astype(jnp.bfloat16), 'mp', scatter_dimension=...]
    pallas_call x0 -> x1, Pallas kernels: none -> 47.9 us  [per_device(): pl.pallas_call(functools.partial(fused, n, n_mp, move_w), out_shape=(jax....]
    dot_general x8 -> x0, matrix products: 11.3 us -> none  [the longest x1 2 us: per_device(): jnp.dot(d_outputs_b, out_weight, preferred_element_type=jnp.float32)]
    unnamed x24 -> x22, local copies, waits for them, and re-layouts: 0.34 us -> 11.4 us
    all_gather x4 -> x0, local copies, waits for them, and re-layouts: 4.95 us -> none  [the longest x1 1.41 us: per_device(): lax.all_gather(key_rows, 'tm', axis=0, tiled=True)]
    convert_element_type x1 -> x0, other arithmetic: 2.62 us -> none  [per_device(): (tangent_x.astype(jnp.float32) + gate_scale * d_summed).astype(jnp.bfloat16)]
  transfers between devices with their start and end apart: 2 -> 0, of which waited for: 2 -> 0; matrix products, arithmetic and copies ran while one was open for 1% -> 0% of each run, Pallas kernels for 0% -> 0%
where the time goes in v1:
time: 61.6 us; the launch traced here: 60.7 us
  Pallas kernels  47.9 us (78%)
  local copies, waits for them, and re-layouts  12.1 us (20%)
  between operations  0.65 us (1%)
    pallas_call x1, Pallas kernels, per_device(): pl.pallas_call(functools.partial(fused, n, n_mp, move_w), out_shape=(jax....  47.9 us
    unnamed x22, local copies, waits for them, and re-layouts  11.4 us

profile of v1, /device:TPU:0, one launch (start us, length us, event | category | flops | bytes accessed | tf_op | source)
XLA Modules:
  0.0 60.7 jit_solution(10359641720281066675)
XLA Ops:
  0.6 0.7 %reshape.7.gate = f32[1,1280]{1,0:T(1,128)S(1)} reshape(f32[1280]{0:T(1024)} %param.19) | data formatting | bytes 10240 | tf_op jit(solution)/shard_map/reshape | solution.py:376
  1.3 0.0 copy-start
  1.3 1.7 %copy-done = bf16[256,5120]{1,0:T(8,128)(2,1)S(1)} copy-done((bf16[256,5120]{1,0:T(8,128)(2,1)S(1)}, bf16[256,5120]{1,0:T(8,128)(2,1)}, u32[]{:S(2)}) %copy-start) | copy-done | bytes 2621464
  3.1 0.0 copy-start.1
  3.1 1.0 %copy-done.1 = bf16[192,1280]{1,0:T(8,128)(2,1)S(1)} copy-done((bf16[192,1280]{1,0:T(8,128)(2,1)S(1)}, bf16[192,1280]{1,0:T(8,128)(2,1)}, u32[]{:S(2)}) %copy-start.1) | copy-done | bytes 491544
  4.1 0.0 copy-start.2
  4.1 1.0 %copy-done.2 = bf16[192,1280]{1,0:T(8,128)(2,1)S(1)} copy-done((bf16[192,1280]{1,0:T(8,128)(2,1)S(1)}, bf16[192,1280]{1,0:T(8,128)(2,1)}, u32[]{:S(2)}) %copy-start.2) | copy-done | bytes 491544
  5.1 0.0 copy-start.3
  5.1 0.9 %copy-done.3 = bf16[192,256]{1,0:T(8,128)(2,1)S(1)} copy-done((bf16[192,256]{1,0:T(8,128)(2,1)S(1)}, bf16[192,256]{1,0:T(8,128)(2,1)}, u32[]{:S(2)}) %copy-start.3) | copy-done | bytes 98328
  6.0 0.0 copy-start.4
  6.0 0.9 %copy-done.4 = bf16[192,256]{1,0:T(8,128)(2,1)S(1)} copy-done((bf16[192,256]{1,0:T(8,128)(2,1)S(1)}, bf16[192,256]{1,0:T(8,128)(2,1)}, u32[]{:S(2)}) %copy-start.4) | copy-done | bytes 98328
  6.9 0.0 copy-start.5
  6.9 0.9 %copy-done.5 = bf16[192,256]{1,0:T(8,128)(2,1)S(1)} copy-done((bf16[192,256]{1,0:T(8,128)(2,1)S(1)}, bf16[192,256]{1,0:T(8,128)(2,1)}, u32[]{:S(2)}) %copy-start.5) | copy-done | bytes 98328
  7.8 0.0 copy-start.6
  7.8 0.9 %copy-done.6 = bf16[192,256]{1,0:T(8,128)(2,1)S(1)} copy-done((bf16[192,256]{1,0:T(8,128)(2,1)S(1)}, bf16[192,256]{1,0:T(8,128)(2,1)}, u32[]{:S(2)}) %copy-start.6) | copy-done | bytes 98328
  8.7 0.0 copy-start.7
  8.7 0.9 %copy-done.7 = bf16[192,256]{1,0:T(8,128)(2,1)S(1)} copy-done((bf16[192,256]{1,0:T(8,128)(2,1)S(1)}, bf16[192,256]{1,0:T(8,128)(2,1)}, u32[]{:S(2)}) %copy-start.7) | copy-done | bytes 98328
  9.6 0.0 copy-start.8
  9.6 0.9 %copy-done.8 = bf16[192,256]{1,0:T(8,128)(2,1)S(1)} copy-done((bf16[192,256]{1,0:T(8,128)(2,1)S(1)}, bf16[192,256]{1,0:T(8,128)(2,1)}, u32[]{:S(2)}) %copy-start.8) | copy-done | bytes 98328
  10.5 0.0 copy-start.9
  10.5 0.7 %copy-done.9 = s32[192]{0:T(256)S(1)} copy-done((s32[192]{0:T(256)S(1)}, s32[192]{0:T(256)}, u32[]{:S(2)}) %copy-start.9) | copy-done | bytes 792
  11.2 47.9 %shard_map.122 = (bf16[192,1280]{1,0:T(8,128)(2,1)S(1)}, bf16[192,1280]{1,0:T(8,128)(2,1)S(1)}) custom-call(bf16[192,256]{1,0:T(8,128)(2,1)S(1)} %copy-done.3, bf16[192,256]{1,0:T(8,128)(2,1)S(1)} %copy-done.4, bf16[192,256]{1,0:T(8,128)(2,1)S(1)} %copy-done.5, bf16[192,256]{1,0:T(8,128)(2,1)S(1)} %copy-done.6, bf16[192,256]{1,0:T(8,128)(2,1)S(1)} %copy-done.7, ...), custom_call_target="tpu_custom_call" | custom-call | tf_op jit(solution)/shard_map/pallas_call | solution.py:341
  59.1 0.8 %copy.15 = bf16[192,1280]{1,0:T(8,128)(2,1)} copy(bf16[192,1280]{1,0:T(8,128)(2,1)S(1)} %get-tuple-element.4) | data formatting | bytes 983040
  59.9 0.8 %copy.16 = bf16[192,1280]{1,0:T(8,128)(2,1)} copy(bf16[192,1280]{1,0:T(8,128)(2,1)S(1)} %get-tuple-element.5) | data formatting | bytes 983040
Async XLA Ops:
  1.3 1.7 %copy-start = (bf16[256,5120]{1,0:T(8,128)(2,1)S(1)}, bf16[256,5120]{1,0:T(8,128)(2,1)}, u32[]{:S(2)}) copy-start(bf16[256,5120]{1,0:T(8,128)(2,1)} %w_hbm.1) | copy-start | bytes 7864324
  3.1 1.0 %copy-start.1 = (bf16[192,1280]{1,0:T(8,128)(2,1)S(1)}, bf16[192,1280]{1,0:T(8,128)(2,1)}, u32[]{:S(2)}) copy-start(bf16[192,1280]{1,0:T(8,128)(2,1)} %x_hbm.1) | copy-start | bytes 1474564
  4.1 1.0 %copy-start.2 = (bf16[192,1280]{1,0:T(8,128)(2,1)S(1)}, bf16[192,1280]{1,0:T(8,128)(2,1)}, u32[]{:S(2)}) copy-start(bf16[192,1280]{1,0:T(8,128)(2,1)} %dx_hbm.1) | copy-start | bytes 1474564
  5.1 0.9 %copy-start.3 = (bf16[192,256]{1,0:T(8,128)(2,1)S(1)}, bf16[192,256]{1,0:T(8,128)(2,1)}, u32[]{:S(2)}) copy-start(bf16[192,256]{1,0:T(8,128)(2,1)} %q_hbm.1) | copy-start | bytes 294916
  6.0 0.9 %copy-start.4 = (bf16[192,256]{1,0:T(8,128)(2,1)S(1)}, bf16[192,256]{1,0:T(8,128)(2,1)}, u32[]{:S(2)}) copy-start(bf16[192,256]{1,0:T(8,128)(2,1)} %dq_hbm.1) | copy-start | bytes 294916
  6.9 0.9 %copy-start.5 = (bf16[192,256]{1,0:T(8,128)(2,1)S(1)}, bf16[192,256]{1,0:T(8,128)(2,1)}, u32[]{:S(2)}) copy-start(bf16[192,256]{1,0:T(8,128)(2,1)} %k_hbm.1) | copy-start | bytes 294916
  7.8 0.9 %copy-start.6 = (bf16[192,256]{1,0:T(8,128)(2,1)S(1)}, bf16[192,256]{1,0:T(8,128)(2,1)}, u32[]{:S(2)}) copy-start(bf16[192,256]{1,0:T(8,128)(2,1)} %v_hbm.1) | copy-start | bytes 294916
  8.7 0.9 %copy-start.7 = (bf16[192,256]{1,0:T(8,128)(2,1)S(1)}, bf16[192,256]{1,0:T(8,128)(2,1)}, u32[]{:S(2)}) copy-start(bf16[192,256]{1,0:T(8,128)(2,1)} %dk_hbm.1) | copy-start | bytes 294916
  9.6 0.9 %copy-start.8 = (bf16[192,256]{1,0:T(8,128)(2,1)S(1)}, bf16[192,256]{1,0:T(8,128)(2,1)}, u32[]{:S(2)}) copy-start(bf16[192,256]{1,0:T(8,128)(2,1)} %dv_hbm.1) | copy-start | bytes 294916
  10.5 0.7 %copy-start.9 = (s32[192]{0:T(256)S(1)}, s32[192]{0:T(256)}, u32[]{:S(2)}) copy-start(s32[192]{0:T(256)} %flags.1) | copy-start | bytes 2308

commit v2 on v1

--- a/solution.py
+++ b/solution.py
@@ -371,7 +371,7 @@
             dma((heads, n_mp)),
         ],
         compiler_params=pltpu.CompilerParams(
-            collective_id=0, has_side_effects=True, vmem_limit_bytes=48 * 1024 * 1024
+            collective_id=0, has_side_effects=True, vmem_limit_bytes=67043328
         ),
     )(q, dq, k, v, dk, dv, flags, w, gate.reshape(1, cols), x, dx)
 

time: 61.6 us -> 54.9 us (0.89)
  local copies, waits for them, and re-layouts: 12.1 us -> 4.97 us
    unnamed x22 -> x2, local copies, waits for them, and re-layouts: 11.4 us -> 3.68 us
where the time goes in v2:
time: 54.9 us; the launch traced here: 54.2 us
  Pallas kernels  48.5 us (88%)
  local copies, waits for them, and re-layouts  4.97 us (9%)
  between operations  0.64 us (1%)
    pallas_call x1, Pallas kernels, per_device(): pl.pallas_call(functools.partial(fused, n, n_mp, move_w), out_shape=(jax....  48.5 us
    unnamed x2, local copies, waits for them, and re-layouts  3.68 us
    reshape x1, local copies, waits for them, and re-layouts, per_device(): gate.reshape(1, cols)  1.29 us

profile of v2, /device:TPU:0, one launch (start us, length us, event | category | flops | bytes accessed | tf_op | source)
XLA Modules:
  0.0 54.2 jit_solution(18280772291193031137)
XLA Ops:
  0.6 1.3 %reshape.7.gate = f32[1,1280]{1,0:T(1,128)} reshape(f32[1280]{0:T(1024)} %param.19) | data formatting | bytes 10240 | tf_op jit(solution)/shard_map/reshape | solution.py:376
  1.9 48.5 %shard_map.122 = (bf16[192,1280]{1,0:T(8,128)(2,1)}, bf16[192,1280]{1,0:T(8,128)(2,1)}) custom-call(bf16[192,256]{1,0:T(8,128)(2,1)} %q_hbm.1, bf16[192,256]{1,0:T(8,128)(2,1)} %dq_hbm.1, bf16[192,256]{1,0:T(8,128)(2,1)} %k_hbm.1, bf16[192,256]{1,0:T(8,128)(2,1)} %v_hbm.1, bf16[192,256]{1,0:T(8,128)(2,1)} %dk_hbm.1, bf16[192,256]{1,0:T(8,128)(2,1)} %dv_hbm.1, ...), custom_call_target="tpu_custom_call" | custom-call | tf_op jit(solution)/shard_map/pallas_call | solution.py:341
  50.5 1.8 %copy.15 = bf16[192,1280]{1,0:T(8,128)(2,1)} copy(bf16[192,1280]{1,0:T(8,128)(2,1)} %get-tuple-element.4) | data formatting | bytes 983040
  52.3 1.8 %copy.16 = bf16[192,1280]{1,0:T(8,128)(2,1)} copy(bf16[192,1280]{1,0:T(8,128)(2,1)} %get-tuple-element.5) | data formatting | bytes 983040

commit v3 on v2

--- a/solution.py
+++ b/solution.py
@@ -192,6 +192,10 @@
             tkv[h, 1, part] = masked(own[3, part, lanes(h)], i)
         if h == 0:
             send_own(0, (2, 3))
+            for g in range(1, heads):
+                send_own(g, (0, 1))
+        else:
+            send_own(h, (2, 3))
     for h in range(heads):
         for i in range(rows // FRAME):
             part = slice(i * FRAME, (i + 1) * FRAME)
@@ -204,7 +208,7 @@
         d_scores = dot_nt(qcat[h], jnp.concatenate([k, tk], axis=1)) * factor
         peak = jnp.max(scores, axis=1, keepdims=True)
         if not first:
-            peak_old = m_s[...]
+            peak_old = m_s[h]
             peak = jnp.maximum(peak_old, peak)
             rescale = jnp.exp((peak_old - peak) * factor)
         weights = jnp.exp((scores - peak) * factor)
@@ -215,22 +219,22 @@
         product_b = product.astype(BF16)
         primal = dot_nn(weights_b, v)
         tangent = dot_nn(product_b, v) + dot_nn(weights_b, tv)
-        m_s[...] = peak
+        m_s[h] = peak
         if first:
-            l_s[...] = total
-            c_s[...] = slope
-            a_s[...] = primal
-            g_s[...] = tangent
+            l_s[h] = total
+            c_s[h] = slope
+            a_s[h] = primal
+            g_s[h] = tangent
         else:
-            l_s[...] = l_s[...] * rescale + total
-            c_s[...] = c_s[...] * rescale + slope
-            a_s[...] = a_s[...] * rescale + primal
-            g_s[...] = g_s[...] * rescale + tangent
+            l_s[h] = l_s[h] * rescale + total
+            c_s[h] = c_s[h] * rescale + slope
+            a_s[h] = a_s[h] * rescale + primal
+            g_s[h] = g_s[h] * rescale + tangent
 
     def finish(h):
-        inverse = 1.0 / l_s[...]
-        outputs = a_s[...] * inverse
-        d_outputs = g_s[...] * inverse - (c_s[...] * inverse) * outputs
+        inverse = 1.0 / l_s[h]
+        outputs = a_s[h] * inverse
+        d_outputs = g_s[h] * inverse - (c_s[h] * inverse) * outputs
         ao[h, 0, 0:rows] = outputs.astype(BF16)
         ao[h, 0, rows : 2 * rows] = d_outputs.astype(BF16)
         for j in list(range(2, n_mp, 2)) + [1]:
@@ -243,20 +247,15 @@
 
     for h in range(heads):
         attend(h, own[0, :, lanes(h)], own[1, :, lanes(h)], tkv[h, 0], tkv[h, 1], True)
-        for s in range(1, half):
+    for s in range(1, half):
+        for h in range(heads):
             for p in range(4):
                 for d in (0, 1):
                     kv_copy(h, d, s, p).wait_recv()
                     if exists(d, s + 1, p):
                         kv_copy(h, d, s + 1, p).start()
-            if h + 1 < heads:
-                if s == 1:
-                    send_own(h + 1, (0, 1))
-                if s == min(2, half - 1):
-                    send_own(h + 1, (2, 3))
             attend(h, *[kv[h, s - 1, p] for p in range(4)], False)
-        if h > 0:
-            relay(h - 1)
+    for h in range(heads):
         for p in range(4):
             kv_copy(h, 0 if p < 2 else 1, half, p).wait_recv()
         attend(h, *[opp[h, p] for p in range(4)], False)
@@ -271,41 +270,42 @@
             return wbuf[j, part, chunk]
         return w_hbm[peers[j], part, chunk]
 
-    def project(h, slots, chunk):
-        attn = jnp.concatenate([ao[h, j] for j in slots], axis=1)
-        weight = jnp.concatenate([w_part(h, j, chunk) for j in slots], axis=0)
+    def project(slots, chunk):
+        attn = jnp.concatenate([ao[h, j] for h, j in slots], axis=1)
+        weight = jnp.concatenate([w_part(h, j, chunk) for h, j in slots], axis=0)
         return dot_nn(attn, weight)
 
-    near = (0, 1)
-    far = tuple(range(2, n_mp))
-    last = heads - 1
-    for h in range(last):
-        for j in range(1, n_mp):
-            if j % 2 == 1:
-                ao_copy(h, j).wait_recv()
-            if move_w:
+    if move_w:
+        for h in range(heads):
+            w_copy(h, 0).wait()
+            for j in range(1, n_mp):
                 w_copy(h, j).wait_recv()
-        if move_w:
-            w_copy(h, 0).wait()
-        for chunk in chunks:
-            part = project(h, near + far, chunk)
-            acc[:, chunk] = part if h == 0 else acc[:, chunk] + part
-    ao_copy(last, 1).wait_recv()
-    if move_w:
-        w_copy(last, 0).wait()
-        for j in range(1, n_mp):
-            w_copy(last, j).wait_recv()
-    for chunk in chunks:
-        part = project(last, near, chunk)
-        acc[:, chunk] = part if last == 0 else acc[:, chunk] + part
     for load in x_loads:
         load.wait()
+    last = heads - 1
+    for h in range(heads):
+        ao_copy(h, 1).wait_recv()
+    near = [(h, j) for h in range(heads) for j in (0, 1)]
+    for chunk in chunks:
+        acc[:, chunk] = project(near, chunk)
+    for h in range(last):
+        relay(h)
+    for h in range(last):
+        for j in range(3, n_mp, 2):
+            ao_copy(h, j).wait_recv()
+    far = [(h, j) for h in range(last) for j in range(2, n_mp)]
+    for chunk in chunks:
+        acc[:, chunk] += project(far, chunk)
     relay(last)
+    even = [(last, j) for j in range(2, n_mp, 2)]
+    for chunk in chunks:
+        acc[:, chunk] += project(even, chunk)
     for j in range(3, n_mp, 2):
         ao_copy(last, j).wait_recv()
+    odd = [(last, j) for j in range(3, n_mp, 2)]
     for chunk in chunks:
-        part = acc[:, chunk] + project(last, far, chunk)
-        scale = gate[:, chunk]
+        part = acc[:, chunk] + project(odd, chunk)
+        scale = gate[chunk].reshape(1, step)
         out[:, chunk] = (xbuf[0, :, chunk].astype(F32) + scale * part[0:rows]).astype(BF16)
         for i in range(rows // FRAME):
             piece = slice(i * FRAME, (i + 1) * FRAME)
@@ -340,7 +340,7 @@
     dma = pltpu.SemaphoreType.DMA
     return pl.pallas_call(
         functools.partial(fused, n, n_mp, move_w),
-        out_shape=(jax.ShapeDtypeStruct(x.shape, BF16), jax.ShapeDtypeStruct(x.shape, BF16)),
+        out_shape=(pltpu.VMEM(x.shape, BF16), pltpu.VMEM(x.shape, BF16)),
         in_specs=[anywhere] * 6
         + [pl.BlockSpec(memory_space=pltpu.SMEM), anywhere if move_w else vmem, vmem]
         + [anywhere] * 2,
@@ -351,11 +351,11 @@
             pltpu.VMEM((heads, 2, rows, HD), BF16),
             pltpu.VMEM((heads, half - 1, 4, 2 * rows, HD), BF16),
             pltpu.VMEM((heads, 4, rows, HD), BF16),
-            pltpu.VMEM((rows, 1), F32),
-            pltpu.VMEM((rows, 1), F32),
-            pltpu.VMEM((rows, 1), F32),
-            pltpu.VMEM((rows, HD), F32),
-            pltpu.VMEM((rows, HD), F32),
+            pltpu.VMEM((heads, rows, 1), F32),
+            pltpu.VMEM((heads, rows, 1), F32),
+            pltpu.VMEM((heads, rows, 1), F32),
+            pltpu.VMEM((heads, rows, HD), F32),
+            pltpu.VMEM((heads, rows, HD), F32),
             pltpu.VMEM((heads, n_mp, 2 * rows, HD), BF16),
             pltpu.VMEM((n_mp, width, cols) if move_w else (1, 16, HD), BF16),
             pltpu.VMEM((2 * rows, cols), F32),
@@ -371,9 +371,9 @@
             dma((heads, n_mp)),
         ],
         compiler_params=pltpu.CompilerParams(
-            collective_id=0, has_side_effects=True, vmem_limit_bytes=67043328
+            collective_id=0, has_side_effects=True, vmem_limit_bytes=65000000
         ),
-    )(q, dq, k, v, dk, dv, flags, w, gate.reshape(1, cols), x, dx)
+    )(q, dq, k, v, dk, dv, flags, w, gate, x, dx)
 
 
 def solution(mesh):

time: 54.9 us -> 46.4 us (0.85); the launches traced: 54.2 us -> 46.3 us
  Pallas kernels: 48.5 us -> 44.1 us
  local copies, waits for them, and re-layouts: 4.97 us -> 1.56 us
    pallas_call x1, Pallas kernels: 48.5 us -> 44.1 us  [per_device(): pl.pallas_call(functools.partial(fused, n, n_mp, move_w), out_shape=(pltp...]
    unnamed x2, local copies, waits for them, and re-layouts: 3.68 us -> 1.56 us
    reshape x1 -> x0, local copies, waits for them, and re-layouts: 1.29 us -> none  [per_device(): gate.reshape(1, cols)]
where the time goes in v3:
time: 46.4 us; the launch traced here: 46.3 us
  Pallas kernels  44.1 us (95%)
  local copies, waits for them, and re-layouts  1.56 us (3%)
  between operations  0.64 us (1%)
    pallas_call x1, Pallas kernels, per_device(): pl.pallas_call(functools.partial(fused, n, n_mp, move_w), out_shape=(pltp...  44.1 us
    unnamed x2, local copies, waits for them, and re-layouts  1.56 us

profile of v3, /device:TPU:0, one launch (start us, length us, event | category | flops | bytes accessed | tf_op | source)
XLA Modules:
  0.0 46.3 jit_solution(4903985065777171775)
XLA Ops:
  0.6 44.1 %shard_map.122 = (bf16[192,1280]{1,0:T(8,128)(2,1)S(1)}, bf16[192,1280]{1,0:T(8,128)(2,1)S(1)}) custom-call(bf16[192,256]{1,0:T(8,128)(2,1)} %q_hbm.1, bf16[192,256]{1,0:T(8,128)(2,1)} %dq_hbm.1, bf16[192,256]{1,0:T(8,128)(2,1)} %k_hbm.1, bf16[192,256]{1,0:T(8,128)(2,1)} %v_hbm.1, bf16[192,256]{1,0:T(8,128)(2,1)} %dk_hbm.1, bf16[192,256]{1,0:T(8,128)(2,1)} %dv_hbm.1, ...), custom_call_target="tpu_custom_call" | custom-call | tf_op jit(solution)/shard_map/pallas_call | solution.py:341
  44.7 0.8 %copy.15 = bf16[192,1280]{1,0:T(8,128)(2,1)} copy(bf16[192,1280]{1,0:T(8,128)(2,1)S(1)} %get-tuple-element.2) | data formatting | bytes 983040
  45.5 0.8 %copy.16 = bf16[192,1280]{1,0:T(8,128)(2,1)} copy(bf16[192,1280]{1,0:T(8,128)(2,1)S(1)} %get-tuple-element.3) | data formatting | bytes 983040

commit v4 on v3

--- a/solution.py
+++ b/solution.py
@@ -51,9 +51,9 @@
     v_hbm,
     dk_hbm,
     dv_hbm,
-    flags,
+    flags_hbm,
     w_hbm,
-    gate,
+    gate_hbm,
     x_hbm,
     dx_hbm,
     out,
@@ -72,8 +72,11 @@
     wbuf,
     acc,
     xbuf,
+    flags,
+    gate,
     own_sem,
     x_sem,
+    small_sem,
     w_local,
     ks,
     kr,
@@ -101,6 +104,7 @@
         pltpu.make_async_copy(src, own.at[i], own_sem.at[i])
         for i, src in enumerate((k_hbm, v_hbm, dk_hbm, dv_hbm, q_hbm, dq_hbm))
     ]
+    loads.append(pltpu.make_async_copy(flags_hbm, flags, small_sem.at[0]))
     for load in loads:
         load.start()
 
@@ -171,6 +175,7 @@
         pltpu.make_async_copy(src, xbuf.at[i], x_sem.at[i])
         for i, src in enumerate((x_hbm, dx_hbm))
     ]
+    x_loads.append(pltpu.make_async_copy(gate_hbm, gate, small_sem.at[1]))
     for load in x_loads:
         load.start()
     for load in loads:
@@ -202,7 +207,7 @@
             qcat[h, part, 0:HD] = masked(own[5, part, lanes(h)], i)
         qcat[h, :, HD : 2 * HD] = own[4, :, lanes(h)]
 
-    def attend(h, k, v, tk, tv, first):
+    def attend(h, k, tk, values, first):
         queries = qcat[h, :, HD : 2 * HD]
         scores = dot_nt(queries, k)
         d_scores = dot_nt(qcat[h], jnp.concatenate([k, tk], axis=1)) * factor
@@ -217,6 +222,7 @@
         slope = jnp.sum(product, axis=1, keepdims=True)
         weights_b = weights.astype(BF16)
         product_b = product.astype(BF16)
+        v, tv = values()
         primal = dot_nn(weights_b, v)
         tangent = dot_nn(product_b, v) + dot_nn(weights_b, tv)
         m_s[h] = peak
@@ -246,7 +252,9 @@
             ao_copy(h, j + 1).start()
 
     for h in range(heads):
-        attend(h, own[0, :, lanes(h)], own[1, :, lanes(h)], tkv[h, 0], tkv[h, 1], True)
+        attend(
+            h, own[0, :, lanes(h)], tkv[h, 0], lambda: (own[1, :, lanes(h)], tkv[h, 1]), True
+        )
     for s in range(1, half):
         for h in range(heads):
             for p in range(4):
@@ -254,11 +262,21 @@
                     kv_copy(h, d, s, p).wait_recv()
                     if exists(d, s + 1, p):
                         kv_copy(h, d, s + 1, p).start()
-            attend(h, *[kv[h, s - 1, p] for p in range(4)], False)
-    for h in range(heads):
-        for p in range(4):
-            kv_copy(h, 0 if p < 2 else 1, half, p).wait_recv()
-        attend(h, *[opp[h, p] for p in range(4)], False)
+            attend(
+                h,
+                kv[h, s - 1, 0],
+                kv[h, s - 1, 2],
+                lambda: (kv[h, s - 1, 1], kv[h, s - 1, 3]),
+                False,
+            )
+    for h in range(heads):
+        def opposite(first_p, second_p):
+            kv_copy(h, 0, half, first_p).wait_recv()
+            kv_copy(h, 1, half, second_p).wait_recv()
+            return opp[h, first_p], opp[h, second_p]
+
+        keys, d_keys = opposite(0, 2)
+        attend(h, keys, d_keys, lambda: opposite(1, 3), False)
         finish(h)
 
     step = 2 * HD if cols % (2 * HD) == 0 else cols
@@ -296,6 +314,15 @@
     far = [(h, j) for h in range(last) for j in range(2, n_mp)]
     for chunk in chunks:
         acc[:, chunk] += project(far, chunk)
+    for h in range(heads):
+        for s in range(1, half + 1):
+            for p in range(4):
+                for d in (0, 1):
+                    if exists(d, s, p):
+                        kv_copy(h, d, s, p).wait_send()
+        if move_w:
+            for j in range(1, n_mp):
+                w_copy(h, j).wait_send()
     relay(last)
     even = [(last, j) for j in range(2, n_mp, 2)]
     for chunk in chunks:
@@ -315,15 +342,8 @@
             d_out[piece, chunk] = (base + scale * delta).astype(BF16)
 
     for h in range(heads):
-        for s in range(1, half + 1):
-            for p in range(4):
-                for d in (0, 1):
-                    if exists(d, s, p):
-                        kv_copy(h, d, s, p).wait_send()
         for j in range(1, n_mp):
             ao_copy(h, j).wait_send()
-            if move_w:
-                w_copy(h, j).wait_send()
 
 
 def per_device(n, n_mp, q, dq, k, v, dk, dv, flags, w, gate, x, dx):
@@ -342,7 +362,7 @@
         functools.partial(fused, n, n_mp, move_w),
         out_shape=(pltpu.VMEM(x.shape, BF16), pltpu.VMEM(x.shape, BF16)),
         in_specs=[anywhere] * 6
-        + [pl.BlockSpec(memory_space=pltpu.SMEM), anywhere if move_w else vmem, vmem]
+        + [anywhere, anywhere if move_w else vmem, anywhere]
         + [anywhere] * 2,
         out_specs=(vmem, vmem),
         scratch_shapes=[
@@ -360,7 +380,10 @@
             pltpu.VMEM((n_mp, width, cols) if move_w else (1, 16, HD), BF16),
             pltpu.VMEM((2 * rows, cols), F32),
             pltpu.VMEM((2, rows, cols), BF16),
+            pltpu.SMEM((rows,), jnp.int32),
+            pltpu.VMEM((cols,), F32),
             dma((6,)),
+            dma((2,)),
             dma((2,)),
             dma((heads,)),
             dma((heads, 2, half, 4)),

time: 46.4 us -> 45.4 us (0.978)
  Pallas kernels: 44.1 us -> 43 us
    pallas_call x1, Pallas kernels: 44.1 us -> 43 us  [per_device(): pl.pallas_call(functools.partial(fused, n, n_mp, move_w), out_shape=(pltp...]
where the time goes in v4:
time: 45.4 us; the launch traced here: 45.2 us
  Pallas kernels  43 us (95%)
  local copies, waits for them, and re-layouts  1.56 us (3%)
  between operations  0.64 us (1%)
    pallas_call x1, Pallas kernels, per_device(): pl.pallas_call(functools.partial(fused, n, n_mp, move_w), out_shape=(pltp...  43 us
    unnamed x2, local copies, waits for them, and re-layouts  1.56 us

profile of v4, /device:TPU:0, one launch (start us, length us, event | category | flops | bytes accessed | tf_op | source)
XLA Modules:
  0.0 45.2 jit_solution(11000964568044804535)
XLA Ops:
  0.6 43.0 %shard_map.122 = (bf16[192,1280]{1,0:T(8,128)(2,1)S(1)}, bf16[192,1280]{1,0:T(8,128)(2,1)S(1)}) custom-call(bf16[192,256]{1,0:T(8,128)(2,1)} %q_hbm.1, bf16[192,256]{1,0:T(8,128)(2,1)} %dq_hbm.1, bf16[192,256]{1,0:T(8,128)(2,1)} %k_hbm.1, bf16[192,256]{1,0:T(8,128)(2,1)} %v_hbm.1, bf16[192,256]{1,0:T(8,128)(2,1)} %dk_hbm.1, bf16[192,256]{1,0:T(8,128)(2,1)} %dv_hbm.1, ...), custom_call_target="tpu_custom_call" | custom-call | tf_op jit(solution)/shard_map/pallas_call | solution.py:361
  43.7 0.8 %copy.15 = bf16[192,1280]{1,0:T(8,128)(2,1)} copy(bf16[192,1280]{1,0:T(8,128)(2,1)S(1)} %get-tuple-element.2) | data formatting | bytes 983040
  44.5 0.8 %copy.16 = bf16[192,1280]{1,0:T(8,128)(2,1)} copy(bf16[192,1280]{1,0:T(8,128)(2,1)S(1)} %get-tuple-element.3) | data formatting | bytes 983040

commit v5 on v4

--- a/solution.py
+++ b/solution.py
@@ -262,6 +262,7 @@
                     kv_copy(h, d, s, p).wait_recv()
                     if exists(d, s + 1, p):
                         kv_copy(h, d, s + 1, p).start()
+        for h in range(heads):
             attend(
                 h,
                 kv[h, s - 1, 0],

time: 45.4 us -> 45.4 us (level)
  no operation moved by 1% of the time
where the time goes in v5:
time: 45.4 us; the launch traced here: 45.3 us
  Pallas kernels  43.1 us (95%)
  local copies, waits for them, and re-layouts  1.56 us (3%)
  between operations  0.64 us (1%)
    pallas_call x1, Pallas kernels, per_device(): pl.pallas_call(functools.partial(fused, n, n_mp, move_w), out_shape=(pltp...  43.1 us
    unnamed x2, local copies, waits for them, and re-layouts  1.56 us

profile of v5, /device:TPU:0, one launch (start us, length us, event | category | flops | bytes accessed | tf_op | source)
XLA Modules:
  0.0 45.3 jit_solution(5654464865421105980)
XLA Ops:
  0.6 43.1 %shard_map.122 = (bf16[192,1280]{1,0:T(8,128)(2,1)S(1)}, bf16[192,1280]{1,0:T(8,128)(2,1)S(1)}) custom-call(bf16[192,256]{1,0:T(8,128)(2,1)} %q_hbm.1, bf16[192,256]{1,0:T(8,128)(2,1)} %dq_hbm.1, bf16[192,256]{1,0:T(8,128)(2,1)} %k_hbm.1, bf16[192,256]{1,0:T(8,128)(2,1)} %v_hbm.1, bf16[192,256]{1,0:T(8,128)(2,1)} %dk_hbm.1, bf16[192,256]{1,0:T(8,128)(2,1)} %dv_hbm.1, ...), custom_call_target="tpu_custom_call" | custom-call | tf_op jit(solution)/shard_map/pallas_call | solution.py:362
  43.7 0.8 %copy.15 = bf16[192,1280]{1,0:T(8,128)(2,1)} copy(bf16[192,1280]{1,0:T(8,128)(2,1)S(1)} %get-tuple-element.2) | data formatting | bytes 983040
  44.5 0.8 %copy.16 = bf16[192,1280]{1,0:T(8,128)(2,1)} copy(bf16[192,1280]{1,0:T(8,128)(2,1)S(1)} %get-tuple-element.3) | data formatting | bytes 983040
